TPU v7x, 32 devices: a whole 2x2x4 slice. The times are simulated.
32 devices in a mesh: row: 8 (over z, x), col: 4 (over y, core).
Axes of the slice: x: 2, y: 2, z: 4, core: 2. Of those that a mesh axis runs over, the one named last changes fastest.
Arguments:
- diagonal_inverses: bfloat16 [24, 2048, 2048], P('row', 'col'), may hold values from -0.125 to 0.125
- column_basis: bfloat16 [24, 2048, 256], P('row', 'col'), may hold values from -6 to 6
- row_basis: bfloat16 [24, 2048, 256], P('row', 'col'), may hold values from -0.125 to 0.125
- transfer: float32 [24, 256, 256], P('row', 'col'), may hold values from -0.375 to 0.375
- coupling: float32 [24, 256, 256], P('row', 'col'), may hold values from -6 to 6
- ranks: int32 [24], P('row'), may hold values from 128 to 256, as said below
Outputs:
- merged: float32 [24, 256, 256], P('row', 'col')
- parent_skeleton: float32 [24, 256, 256], P('row', 'col')
Inputs may be any that keep to these rules, and one draw needn't show every extreme that they name: `ranks`: each rank is 128 or 256; both occur in every draw.
All inputs are finite; a program needn't handle non-finite values.
Results may differ from a plain program's by a relative error of at most 0.0021.
Values may be sent and summed in bfloat16 or wider, within the bound.
A program may use at most 64 MiB of HBM per device.

v0:
```python
import jax
import jax.numpy as jnp
from jax import lax
from jax.sharding import PartitionSpec as P

BIT = 2


def swapped(block, axis, bit):
    count = lax.axis_size(axis)
    route = []
    for low in range(count):
        high = low | 1 << bit
        if high != low and high < count:
            route += [(low, high), (high, low)]
    return lax.ppermute(block, axis, route)


def shards(diagonal_inverses, column_basis, row_basis, transfer, coupling, ranks):
    rank_width = transfer.shape[2]
    part_rows = transfer.shape[1]
    highest = lax.Precision.HIGHEST
    live_cols = jnp.arange(rank_width, dtype=jnp.int32)[None, :] < ranks[:, None]
    left_factor_basis = jnp.where(live_cols[:, None, :], column_basis, jnp.zeros_like(column_basis))
    right_factor_basis = jnp.where(live_cols[:, None, :], row_basis, jnp.zeros_like(row_basis))
    eliminated_part = jnp.einsum(
        "nmp,npr->nmr",
        diagonal_inverses,
        lax.all_gather(left_factor_basis, "col", axis=1, tiled=True),
        preferred_element_type=jnp.float32,
    ).astype(jnp.bfloat16)
    skeleton = jnp.transpose(
        lax.psum_scatter(
            jnp.einsum(
                "hgp,hgd->phd",
                right_factor_basis,
                eliminated_part,
                preferred_element_type=jnp.float32,
            ),
            "col",
            scatter_dimension=0,
            tiled=True,
        ),
        (1, 0, 2),
    )
    offset_rows = lax.axis_index("col") * part_rows
    active_rows = lax.dynamic_slice_in_dim(live_cols, offset_rows, part_rows, 1)
    masked = transfer * active_rows[:, :, None].astype(jnp.float32)
    masked_sib = swapped(masked, "row", BIT)
    complete_local_block, whole_sib = (
        lax.all_gather(masked, "col", axis=1, tiled=True),
        lax.all_gather(masked_sib, "col", axis=1, tiled=True),
    )
    merged = jnp.einsum("nij,njk->nik", skeleton, complete_local_block, precision=highest)
    merged = merged + jnp.einsum("nij,njk->nik", coupling, whole_sib, precision=highest)
    own_term = jnp.transpose(
        lax.psum_scatter(
            jnp.einsum("nji,njk->ink", masked, merged, precision=highest),
            "col",
            scatter_dimension=0,
            tiled=True,
        ),
        (1, 0, 2),
    )
    parent = own_term + swapped(own_term, "row", BIT)
    return (merged, parent)


def solution(mesh):
    placed = (
        P("row", "col", None),
        P("row", "col", None),
        P("row", "col", None),
        P("row", "col", None),
        P("row", "col", None),
        P("row"),
    )
    return jax.shard_map(
        shards,
        mesh=mesh,
        in_specs=placed,
        out_specs=(P("row", "col", None), P("row", "col", None)),
        check_vma=False,
    )
```

profile of v0, /device:TPU:0, one launch (start us, length us, event | category | flops | bytes accessed | tf_op | source)
XLA Modules:
  0.0 138.4 jit_solution(1713739336658735654)
XLA Ops:
  7.2 0.8 iota_compare_fusion
  8.0 2.1 %broadcast_select_fusion = bf16[3,512,256]{2,1,0:T(8,128)(2,1)} fusion(bf16[3,512,256]{2,1,0:T(8,128)(2,1)} %param.7, pred[3,256]{1,0:T(4,128)(4,1)S(1)} %iota_compare_fusion), kind=kLoop, calls=%fused_computation.7 | loop fusion | flops 393216 | bytes 1573632 | tf_op jit(solution)/shard_map/jit(_where)/select_n | solution.py:24
  10.1 0.0 reduce-scatter.2.cloned.1.call-start
  10.2 31.3 %all-gather.2.cloned.1.call-done = bf16[3,2048,256]{2,1,0:T(8,128)(2,1)} async-done(((bf16[3,512,256]{2,1,0:T(8,128)(2,1)}), bf16[3,2048,256]{2,1,0:T(8,128)(2,1)}) %all-gather.2.cloned.1.call-update) | async-done | bytes 3145744 | tf_op jit(solution)/shard_map/all_gather | solution.py:29
  41.5 7.1 %convolution_bitcast_fusion = f32[256,3,256]{2,0,1:T(8,128)} fusion(bf16[3,2048,256]{2,1,0:T(8,128)(2,1)} %all-gather.2.cloned.1.call-done, bf16[3,512,2048]{2,1,0:T(8,128)(2,1)} %param.6, bf16[3,512,256]{2,1,0:T(8,128)(2,1)} %param.8, pred[3,256]{1,0:T(4,128)(4,1)S(1)} %iota_compare_fusion), kind=kOutput, calls=%fused_computation.1 | convolution fusion | flops 1812725760 | bytes 11010816 | tf_op jit(solution)/shard_map/hgp,hgd->phd/dot_general | solution.py:34
  48.6 0.0 all-reduce.3.cloned.1.call-start
  48.7 0.1 dynamic-slice_convert_fusion
  48.8 0.1 broadcast_multiply_fusion
  48.9 2.5 %collective-permute-start = (f32[3,64,256]{2,1,0:T(8,128)S(1)}, f32[3,64,256]{2,1,0:T(8,128)S(1)}, u32[]{:S(2)}, u32[]{:S(2)}) collective-permute-start(f32[3,64,256]{2,1,0:T(8,128)S(1)} %broadcast_multiply_fusion), channel_id=1, source_target_pairs={{0,16},{16,0},{4,20},{20,4},{8,24},{24,8},{12,28},{28,12},{1,17},{... | collective-permute-start | bytes 589832 | tf_op jit(solution)/shard_map/ppermute | solution.py:16
  51.3 8.3 %all_gather.10 = f32[3,256,256]{2,1,0:T(8,128)S(1)} all-gather(f32[3,64,256]{2,1,0:T(8,128)S(1)} %broadcast_multiply_fusion), channel_id=1, replica_groups=mesh['row'=8,'col'=4] {'col'}, dimensions={1}, use_global_device_ids=true | all-gather | bytes 983040 | tf_op jit(solution)/shard_map/all_gather | solution.py:51
  59.6 1.4 %collective-permute-done = f32[3,64,256]{2,1,0:T(8,128)S(1)} collective-permute-done((f32[3,64,256]{2,1,0:T(8,128)S(1)}, f32[3,64,256]{2,1,0:T(8,128)S(1)}, u32[]{:S(2)}, u32[]{:S(2)}) %collective-permute-start) | collective-permute-done | bytes 196640 | tf_op jit(solution)/shard_map/ppermute | solution.py:16
  61.1 10.0 %all_gather.11 = f32[3,256,256]{2,1,0:T(8,128)S(1)} all-gather(f32[3,64,256]{2,1,0:T(8,128)S(1)} %collective-permute-done), channel_id=1, replica_groups=mesh['row'=8,'col'=4] {'col'}, dimensions={1}, use_global_device_ids=true | all-gather | bytes 983040 | tf_op jit(solution)/shard_map/all_gather | solution.py:52
  71.1 2.1 %reduce-scatter.2.cloned.1.call-done = f32[64,3,256]{2,0,1:T(8,128)} async-done(((f32[256,3,256]{2,0,1:T(8,128)}), f32[64,3,256]{2,0,1:T(8,128)}) %reduce-scatter.2.cloned.1.call-update) | async-done | bytes 196624 | tf_op jit(solution)/shard_map/reduce_scatter | solution.py:33
  73.2 1.5 %fusion.4 = f32[3,64,256]{2,1,0:T(8,128)S(1)} fusion(f32[3,256,256]{2,1,0:T(8,128)S(1)} %all_gather.10, f32[64,3,256]{2,0,1:T(8,128)} %reduce-scatter.2.cloned.1.call-done), kind=kOutput, calls=%fused_computation.10 | convolution fusion | flops 150994944 | bytes 1179648 | tf_op jit(solution)/shard_map/nij,njk->nik/dot_general | solution.py:54
  74.7 0.6 fusion
  75.4 0.8 convolution_bitcast_fusion.1
  76.2 1.4 copy.9
  77.6 0.6 dynamic-slice
  78.8 36.0 %all-reduce.3.cloned.1.call-done = f32[256,3,256]{2,1,0:T(4,128)} async-done(((f32[256,3,256]{2,1,0:T(4,128)}), f32[256,3,256]{2,1,0:T(4,128)}) %all-reduce.3.cloned.1.call-update) | async-done | bytes 786448
  114.8 1.0 dynamic-slice_bitcast_fusion
  115.8 2.5 %collective-permute-start.1 = (f32[3,64,256]{2,0,1:T(4,128)S(1)}, f32[3,64,256]{2,0,1:T(4,128)S(1)}, u32[]{:S(2)}, u32[]{:S(2)}) collective-permute-start(f32[3,64,256]{2,0,1:T(4,128)S(1)} %dynamic-slice_bitcast_fusion), channel_id=1, source_target_pairs={{0,16},{16,0},{4,20},{20,4},{8,24},{24,8},{12,28},{28,12},{1,17},{... | collective-permute-start | bytes 589832 | tf_op jit(solution)/shard_map/ppermute | solution.py:16
  118.3 11.8 %collective-permute-done.1 = f32[3,64,256]{2,0,1:T(4,128)S(1)} collective-permute-done((f32[3,64,256]{2,0,1:T(4,128)S(1)}, f32[3,64,256]{2,0,1:T(4,128)S(1)}, u32[]{:S(2)}, u32[]{:S(2)}) %collective-permute-start.1) | collective-permute-done | bytes 196640 | tf_op jit(solution)/shard_map/ppermute | solution.py:16
  130.1 1.0 fusion.14
  131.1 0.7 copy.10
  (12 shorter events, 0.1 us)
Async XLA Ops:
  7.2 67.6 %copy-start = (f32[3,64,256]{2,1,0:T(8,128)S(1)}, f32[3,64,256]{2,1,0:T(8,128)}, u32[]{:S(2)}) copy-start(f32[3,64,256]{2,1,0:T(8,128)} %param.10) | copy-start | bytes 589828
  7.2 34.3 %all-gather.2.cloned.1.call-start = ((), (), s32[]{:S(2)}) async-start(), calls=%async_computation.1 | async-start | bytes 3932160 | tf_op jit(solution)/shard_map/all_gather | solution.py:29
  10.1 38.7 %copy-start.2 = (f32[3,64,256]{2,1,0:T(8,128)S(1)}, f32[3,64,256]{2,1,0:T(8,128)}, u32[]{:S(2)}) copy-start(f32[3,64,256]{2,1,0:T(8,128)} %param.9) | copy-start | bytes 589828
  10.1 63.1 %reduce-scatter.2.cloned.1.call-start = ((), (), s32[]{:S(2)}) async-start(), calls=%async_computation.2 | async-start | bytes 983040 | tf_op jit(solution)/shard_map/reduce_scatter | solution.py:33
  48.6 66.2 %all-reduce.3.cloned.1.call-start = ((), (), s32[]{:S(2)}) async-start(), calls=%async_computation.3 | async-start | bytes 2097152
  48.9 12.2 %collective-permute-start = (f32[3,64,256]{2,1,0:T(8,128)S(1)}, f32[3,64,256]{2,1,0:T(8,128)S(1)}, u32[]{:S(2)}, u32[]{:S(2)}) collective-permute-start(f32[3,64,256]{2,1,0:T(8,128)S(1)} %broadcast_multiply_fusion), channel_id=1, source_target_pairs={{0,16},{16,0},{4,20},{20,4},{8,24},{24,8},{12,28},{28,12},{1,17},{... | collective-permute-start | bytes 589832 | tf_op jit(solution)/shard_map/ppermute | solution.py:16
  71.1 6.5 %copy-start.3 = (u32[32]{0:T(128)S(1)}, u32[32]{0:T(128)}, u32[]{:S(2)}) copy-start(u32[32]{0:T(128)} %constant.20) | copy-start | bytes 388
  75.4 56.5 %copy-start.1 = (f32[3,64,256]{2,1,0:T(8,128)}, f32[3,64,256]{2,1,0:T(8,128)S(1)}, u32[]{:S(2)}) copy-start(f32[3,64,256]{2,1,0:T(8,128)S(1)} %fusion) | copy-start | bytes 589828
  115.8 14.3 %collective-permute-start.1 = (f32[3,64,256]{2,0,1:T(4,128)S(1)}, f32[3,64,256]{2,0,1:T(4,128)S(1)}, u32[]{:S(2)}, u32[]{:S(2)}) collective-permute-start(f32[3,64,256]{2,0,1:T(4,128)S(1)} %dynamic-slice_bitcast_fusion), channel_id=1, source_target_pairs={{0,16},{16,0},{4,20},{20,4},{8,24},{24,8},{12,28},{28,12},{1,17},{... | collective-permute-start | bytes 589832 | tf_op jit(solution)/shard_map/ppermute | solution.py:16
Sparse Core Ops, SparseCore 0:
  10.2 31.2 all-gather.1
  48.7 24.3 reduce-scatter.1
  77.7 37.0 all-reduce.2
where the time goes:
time: 139 us; the launch traced here: 138 us
  waiting for transfers between devices  82.7 us (59%)
  blocking collectives  18.3 us (13%)
  between operations  14.5 us (10%)
  matrix products  10.1 us (7%)
  starting transfers between devices  5.07 us (4%)
  other arithmetic  4.03 us (3%)
  local copies, waits for them, and re-layouts  3.68 us (3%)
    unnamed x4, waiting for transfers between devices  36 us
    all_gather x1, waiting for transfers between devices, shards(): lax.all_gather(left_factor_basis, 'col', axis=1, tiled=True)  31.3 us
    ppermute x2, waiting for transfers between devices, swapped(): return lax.ppermute(block, axis, route)  13.3 us
    all_gather x1, blocking collectives, shards(): lax.all_gather(masked_sib, 'col', axis=1, tiled=True)  9.98 us
    all_gather x1, blocking collectives, shards(): lax.all_gather(masked, 'col', axis=1, tiled=True)  8.3 us
    dot_general x1, matrix products, shards(): jnp.einsum('hgp,hgd->phd', right_factor_basis, eliminated_part, preferred...  7.12 us
    ppermute x2, starting transfers between devices, swapped(): return lax.ppermute(block, axis, route)  4.94 us
  transfers between devices with their start and end apart: 5, of which 5 were waited for; matrix products, arithmetic and copies ran while one was open for 1% of the time, Pallas kernels for 0%

commit v1 on v0

v1 whole, which is shorter than its diff:
```python
import jax
import jax.numpy as jnp
from jax import lax
from jax.experimental import pallas as pl
from jax.experimental.pallas import tpu as pltpu
from jax.sharding import PartitionSpec as P

BIT = 2
MESH = pl.DeviceIdType.MESH
LY, LC, LF, TY, TC, TF, TZ, TG, ZC, ZG, SC, SY, PC, PY, PZ = range(15)


def kernel(
    ranks_ref, d_ref, l_ref, r_ref, t_ref, k_ref, merged_ref, parent_ref,
    dv, lv, rv, tv, kv, tw, zw, sbuf, sgot, ysend, ygot, pbuf, pgot, pysend, pygot,
    esend, egot, mv, pv, send_sem, recv_sem, d_sem, loc_sem, out_sem,
):
    nodes, block, _ = l_ref.shape
    part = t_ref.shape[1]
    width = t_ref.shape[2]
    highest = lax.Precision.HIGHEST
    c = lax.axis_index("col")
    r = lax.axis_index("row")
    core = lax.rem(c, 2)
    y = lax.div(c, 2)
    cp = c + 1 - 2 * core
    yp = c + 2 - 4 * y
    high = lax.rem(lax.div(r, 1 << BIT), 2)
    sib = r + (1 << BIT) - (2 << BIT) * high
    other = 1 - y

    to_core = {"col": cp}
    to_y = {"col": yp}
    to_z = {"row": sib}
    slots = (c, cp, yp, cp + yp - c)

    def rows_of(index):
        return pl.ds(pl.multiple_of(index * part, part), part)

    t_in = pltpu.make_async_copy(t_ref, tv, loc_sem.at[0])
    t_in.start()
    l_in, d_in = [], []
    for n in range(nodes):
        cp_l = pltpu.make_async_copy(l_ref.at[n], lv.at[n, pl.ds(0, block)], d_sem.at[n, 4])
        cp_l.start()
        l_in.append(cp_l)
        for s in range(4):
            src = d_ref.at[n, :, pl.ds(pl.multiple_of(slots[s] * block, block), block)]
            one = pltpu.make_async_copy(src, dv.at[n, :, pl.ds(s * block, block)], d_sem.at[n, s])
            one.start()
            d_in.append(one)
    r_in = pltpu.make_async_copy(r_ref, rv, loc_sem.at[1])
    r_in.start()
    k_in = pltpu.make_async_copy(k_ref, kv, loc_sem.at[2])
    k_in.start()

    barrier = pltpu.get_barrier_semaphore()
    for device in (to_core, to_y, to_z):
        pl.semaphore_signal(barrier, inc=1, device_id=device, device_id_type=MESH)

    t_in.wait()
    row_at = lax.broadcasted_iota(jnp.int32, (part, width), 0) + c * part
    col_at = lax.broadcasted_iota(jnp.int32, (part, width), 1)
    for n in range(nodes):
        tw[n, rows_of(c), :] = jnp.where(row_at < ranks_ref[n], tv[n], 0.0)
    pl.semaphore_wait(barrier, 3)

    sent = []

    def copy(kind, n, src, dst, device):
        return pltpu.make_async_remote_copy(
            src_ref=src, dst_ref=dst, send_sem=send_sem.at[kind, n], recv_sem=recv_sem.at[kind, n],
            device_id=device, device_id_type=MESH,
        )

    def send(kind, n, src, dst, device):
        one = copy(kind, n, src, dst, device)
        one.start()
        sent.append(one)

    def got(kind, n, ref, device):
        copy(kind, n, ref, ref, device).wait_recv()

    def slot(n, s):
        return lv.at[n, pl.ds(s * block, block)]

    def strip(buf, n, index):
        return buf.at[n, rows_of(index)]

    for n in range(nodes):
        send(TY, n, strip(tw, n, c), strip(tw, n, c), to_y)
        send(LY, n, l_ref.at[n], slot(n, 2), to_y)
        send(LC, n, l_ref.at[n], slot(n, 1), to_core)
        send(TZ, n, strip(tw, n, c), strip(zw, n, c), to_z)
        send(TC, n, strip(tw, n, c), strip(tw, n, c), to_core)

    def times(n, first, count):
        span = pl.ds(first * block, count * block)
        return jnp.dot(dv[n, :, span], lv[n, span, :], preferred_element_type=jnp.float32)

    def eliminate(n):
        got(TY, n, strip(tw, n, yp), to_y)
        send(TG, n, strip(tw, n, yp), strip(zw, n, yp), to_z)
        send(TF, n, strip(tw, n, yp), strip(tw, n, yp), to_core)
        l_in[n].wait()
        for s in range(4):
            d_in[4 * n + s].wait()
        got(LC, n, slot(n, 1), to_core)
        total = times(n, 0, 2)
        got(LY, n, slot(n, 2), to_y)
        send(LF, n, slot(n, 2), slot(n, 3), to_core)
        total = total + times(n, 2, 1)
        got(LF, n, slot(n, 3), to_core)
        total = total + times(n, 3, 1)
        skeleton = lax.dot_general(
            rv[n], total.astype(jnp.bfloat16), (((0,), (0,)), ((), ())), preferred_element_type=jnp.float32
        )
        sbuf[n] = skeleton.reshape(2, 2, part, width)
        send(SC, n, sbuf.at[n, :, 1 - core], sgot.at[n], to_core)

    def reduce_chip(n):
        got(SC, n, sgot.at[n], to_core)
        ysend[n] = (sbuf[n, other, core] + sgot[n, other]).astype(ysend.dtype)
        send(SY, n, ysend.at[n], ygot.at[n], to_y)

    def hand_on_sibling(n):
        got(TZ, n, strip(zw, n, c), to_z)
        send(ZC, n, strip(zw, n, c), strip(zw, n, c), to_core)
        got(TG, n, strip(zw, n, yp), to_z)
        send(ZG, n, strip(zw, n, yp), strip(zw, n, yp), to_core)

    def couple(n):
        got(ZC, n, strip(zw, n, cp), to_core)
        got(ZG, n, strip(zw, n, slots[3]), to_core)
        got(TC, n, strip(tw, n, cp), to_core)
        got(TF, n, strip(tw, n, slots[3]), to_core)
        mv[n] = jnp.dot(kv[n], zw[n], precision=highest, preferred_element_type=jnp.float32)

    outs = []

    def merge(n):
        got(SY, n, ygot.at[n], to_y)
        mine = sbuf[n, y, core] + sgot[n, y] + ygot[n].astype(jnp.float32)
        live = (row_at < ranks_ref[n]) & (col_at < ranks_ref[n])
        mine = jnp.where(live, mine, 0.0)
        merged = mv[n] + jnp.dot(mine, tw[n], precision=highest, preferred_element_type=jnp.float32)
        mv[n] = merged
        own = lax.dot_general(
            tw[n, rows_of(c), :], merged, (((0,), (0,)), ((), ())), precision=highest,
            preferred_element_type=jnp.float32,
        )
        pbuf[n] = own.reshape(2, 2, part, width)
        send(PC, n, pbuf.at[n, :, 1 - core], pgot.at[n], to_core)
        one = pltpu.make_async_copy(mv.at[n], merged_ref.at[n], out_sem.at[0, n])
        one.start()
        outs.append(one)

    def parent_chip(n):
        got(PC, n, pgot.at[n], to_core)
        pysend[n] = (pbuf[n, other, core] + pgot[n, other]).astype(pysend.dtype)
        send(PY, n, pysend.at[n], pygot.at[n], to_y)

    def parent_own(n):
        got(PY, n, pygot.at[n], to_y)
        own = pbuf[n, y, core] + pgot[n, y] + pygot[n].astype(jnp.float32)
        pv[n] = own
        esend[n] = own.astype(esend.dtype)
        send(PZ, n, esend.at[n], egot.at[n], to_z)

    def parent_all(n):
        got(PZ, n, egot.at[n], to_z)
        pv[n] = pv[n] + egot[n].astype(jnp.float32)
        one = pltpu.make_async_copy(pv.at[n], parent_ref.at[n], out_sem.at[1, n])
        one.start()
        outs.append(one)

    r_in.wait()
    for n in range(nodes):
        eliminate(n)
        if n >= 1:
            reduce_chip(n - 1)
            hand_on_sibling(n - 1)
    k_in.wait()
    hand_on_sibling(nodes - 1)
    for n in range(nodes - 1):
        couple(n)
    reduce_chip(nodes - 1)
    couple(nodes - 1)
    for n in range(nodes):
        merge(n)
        if n >= 1:
            parent_chip(n - 1)
    for n in range(nodes - 1):
        parent_own(n)
    parent_chip(nodes - 1)
    for n in range(nodes - 1):
        parent_all(n)
    parent_own(nodes - 1)
    parent_all(nodes - 1)
    for one in sent:
        one.wait_send()
    for one in outs:
        one.wait()


def shards(diagonal_inverses, column_basis, row_basis, transfer, coupling, ranks):
    nodes, block, whole = diagonal_inverses.shape
    part, width = transfer.shape[1:]
    f32, bf16 = jnp.float32, jnp.bfloat16
    skeleton_link, parent_link, sibling_link = f32, f32, f32
    anywhere = pl.BlockSpec(memory_space=pl.ANY)
    strips = (nodes, part, width)
    square = (nodes, width, width)
    quads = (nodes, 2, 2, part, width)
    pairs = (nodes, 2, part, width)
    shape = jax.ShapeDtypeStruct(strips, f32)
    return pl.pallas_call(
        kernel,
        out_shape=(shape, shape),
        in_specs=[pl.BlockSpec(memory_space=pltpu.SMEM)] + [anywhere] * 5,
        out_specs=(anywhere, anywhere),
        scratch_shapes=[
            pltpu.VMEM((nodes, block, whole), bf16),
            pltpu.VMEM((nodes, whole, width), bf16),
            pltpu.VMEM((nodes, block, width), bf16),
            pltpu.VMEM(strips, f32),
            pltpu.VMEM(strips, f32),
            pltpu.VMEM(square, f32),
            pltpu.VMEM(square, f32),
            pltpu.VMEM(quads, f32),
            pltpu.VMEM(pairs, f32),
            pltpu.VMEM(strips, skeleton_link),
            pltpu.VMEM(strips, skeleton_link),
            pltpu.VMEM(quads, f32),
            pltpu.VMEM(pairs, f32),
            pltpu.VMEM(strips, parent_link),
            pltpu.VMEM(strips, parent_link),
            pltpu.VMEM(strips, sibling_link),
            pltpu.VMEM(strips, sibling_link),
            pltpu.VMEM(strips, f32),
            pltpu.VMEM(strips, f32),
            pltpu.SemaphoreType.DMA((15, nodes)),
            pltpu.SemaphoreType.DMA((15, nodes)),
            pltpu.SemaphoreType.DMA((nodes, 5)),
            pltpu.SemaphoreType.DMA((3,)),
            pltpu.SemaphoreType.DMA((2, nodes)),
        ],
        compiler_params=pltpu.CompilerParams(collective_id=0, has_side_effects=True),
    )(ranks, diagonal_inverses, column_basis, row_basis, transfer, coupling)


def solution(mesh):
    placed = (P("row", "col", None),) * 5 + (P("row"),)
    return jax.shard_map(
        shards,
        mesh=mesh,
        in_specs=placed,
        out_specs=(P("row", "col", None), P("row", "col", None)),
        check_vma=False,
    )
```

time: 139 us -> 55.1 us (0.40)
  waiting for transfers between devices: 82.7 us -> 0 us
  Pallas kernels: 0 us -> 51.1 us
  blocking collectives: 18.3 us -> 0 us
  between operations: 14.5 us -> 0.64 us
  matrix products: 10.1 us -> 0 us
  starting transfers between devices: 5.07 us -> 0 us
  other arithmetic: 4.03 us -> 0 us
    pallas_call x0 -> x1, Pallas kernels: none -> 51.1 us  [shards(): pl.pallas_call(kernel, out_shape=(shape, shape), in_specs=[pl.BlockSpec(m...]
    unnamed x4 -> x0, waiting for transfers between devices: 36 us -> none
    all_gather x1 -> x0, waiting for transfers between devices: 31.3 us -> none  [shards(): lax.all_gather(left_factor_basis, 'col', axis=1, tiled=True)]
    all_gather x2 -> x0, blocking collectives: 18.3 us -> none  [the longest x1 9.98 us: shards(): lax.all_gather(masked_sib, 'col', axis=1, tiled=True)]
    ppermute x2 -> x0, waiting for transfers between devices: 13.3 us -> none  [swapped(): return lax.ppermute(block, axis, route)]
    dot_general x4 -> x0, matrix products: 10.1 us -> none  [the longest x1 7.12 us: shards(): jnp.einsum('hgp,hgd->phd', right_factor_basis, eliminated_part, preferred...]
    ppermute x2 -> x0, starting transfers between devices: 4.94 us -> none  [swapped(): return lax.ppermute(block, axis, route)]
    transpose x2 -> x0, local copies, waits for them, and re-layouts: 2.35 us -> none  [the longest x1 1.36 us: shards(): jnp.einsum('nji,njk->ink', masked, merged, precision=highest)]
  transfers between devices with their start and end apart: 5 -> 0, of which waited for: 5 -> 0; matrix products, arithmetic and copies ran while one was open for 1% -> 0% of each run, Pallas kernels for 0% -> 0%
where the time goes in v1:
time: 55.1 us; the launch traced here: 55 us
  Pallas kernels  51.1 us (93%)
  local copies, waits for them, and re-layouts  3.23 us (6%)
  between operations  0.64 us (1%)
    pallas_call x1, Pallas kernels, shards(): pl.pallas_call(kernel, out_shape=(shape, shape), in_specs=[pl.BlockSpec(m...  51.1 us
    unnamed x2, local copies, waits for them, and re-layouts  3.23 us

profile of v1, /device:TPU:0, one launch (start us, length us, event | category | flops | bytes accessed | tf_op | source)
XLA Modules:
  0.0 55.0 jit_solution(12220338556983079577)
XLA Ops:
  0.6 51.1 %shard_map.77 = (f32[3,64,256]{2,1,0:T(8,128)}, f32[3,64,256]{2,1,0:T(8,128)}) custom-call(s32[3]{0:T(128)} %ranks_ref.1, bf16[3,512,2048]{2,1,0:T(8,128)(2,1)} %d_ref.1, bf16[3,512,256]{2,1,0:T(8,128)(2,1)} %l_ref.1, bf16[3,512,256]{2,1,0:T(8,128)(2,1)} %r_ref.1, f32[3,64,256]{2,1,0:T(8,128)} %t_ref.1, f32[3,64,256]{2,1,0:T(8,128)} %k_ref.1), custom_call_target="tpu_custom_call" | custom-call | tf_op jit(solution)/shard_map/pallas_call | solution.py:217
  51.7 1.6 %copy.10 = f32[3,64,256]{2,1,0:T(8,128)} copy(f32[3,64,256]{2,1,0:T(8,128)} %get-tuple-element.4) | data formatting | bytes 393216
  53.4 1.6 %copy.11 = f32[3,64,256]{2,1,0:T(8,128)} copy(f32[3,64,256]{2,1,0:T(8,128)} %get-tuple-element.5) | data formatting | bytes 393216

commit v2 on v1

--- a/solution.py
+++ b/solution.py
@@ -7,7 +7,7 @@
 
 BIT = 2
 MESH = pl.DeviceIdType.MESH
-LY, LC, LF, TY, TC, TF, TZ, TG, ZC, ZG, SC, SY, PC, PY, PZ = range(15)
+LY, LC, LF, TY, TC, TF, TZ, TG, ZC, ZG, SC, SY, PC, PY, PZ, MY, MF = range(17)
 
 
 def kernel(
@@ -18,7 +18,6 @@
     nodes, block, _ = l_ref.shape
     part = t_ref.shape[1]
     width = t_ref.shape[2]
-    highest = lax.Precision.HIGHEST
     c = lax.axis_index("col")
     r = lax.axis_index("row")
     core = lax.rem(c, 2)
@@ -34,16 +33,81 @@
     to_z = {"row": sib}
     slots = (c, cp, yp, cp + yp - c)
 
+    def halves(x):
+        top = x.astype(jnp.bfloat16)
+        return top, (x - top.astype(jnp.float32)).astype(jnp.bfloat16)
+
+    def product(a, b, dims):
+        a_top, a_low = halves(a)
+        b_top, b_low = halves(b)
+        lhs = jnp.concatenate([a_top, a_low, a_top], axis=dims[0])
+        rhs = jnp.concatenate([b_top, b_top, b_low], axis=dims[1])
+        return lax.dot_general(
+            lhs, rhs, (((dims[0],), (dims[1],)), ((), ())), preferred_element_type=jnp.float32
+        )
+
     def rows_of(index):
         return pl.ds(pl.multiple_of(index * part, part), part)
 
     t_in = pltpu.make_async_copy(t_ref, tv, loc_sem.at[0])
     t_in.start()
+    barrier = pltpu.get_barrier_semaphore()
+    for device in (to_core, to_y, to_z):
+        pl.semaphore_signal(barrier, inc=1, device_id=device, device_id_type=MESH)
+
+    row_at = lax.broadcasted_iota(jnp.int32, (part, width), 0) + c * part
+    col_at = lax.broadcasted_iota(jnp.int32, (part, width), 1)
+    pl.semaphore_wait(barrier, 3)
+
+    sent = []
+
+    def copy(kind, n, src, dst, device):
+        return pltpu.make_async_remote_copy(
+            src_ref=src, dst_ref=dst, send_sem=send_sem.at[kind, n], recv_sem=recv_sem.at[kind, n],
+            device_id=device, device_id_type=MESH,
+        )
+
+    def send(kind, n, src, dst, device):
+        one = copy(kind, n, src, dst, device)
+        one.start()
+        sent.append(one)
+
+    def got(kind, n, ref, device):
+        copy(kind, n, ref, ref, device).wait_recv()
+
+    def slot(n, s):
+        return lv.at[n, pl.ds(s * block, block)]
+
+    def strip(buf, n, index):
+        return buf.at[n, rows_of(index)]
+
+    half = block // 2
+    last = nodes - 1
+
+    def piece(n, s, first):
+        return lv.at[n, pl.ds(s * block + first, half)]
+
+    def send_basis(n):
+        send(LY, n, l_ref.at[n], slot(n, 2), to_y)
+
+    send_basis(0)
+    send(LC, 0, l_ref.at[0], slot(0, 1), to_core)
+    t_in.wait()
+    for n in range(nodes):
+        tw[n, rows_of(c), :] = jnp.where(row_at < ranks_ref[n], tv[n], 0.0)
+    for n in range(nodes):
+        send(TY, n, strip(tw, n, c), strip(tw, n, c), to_y)
+        send(TZ, n, strip(tw, n, c), strip(zw, n, c), to_z)
+        send(TC, n, strip(tw, n, c), strip(tw, n, c), to_core)
+    for n in range(1, nodes - 1):
+        send_basis(n)
     l_in, d_in = [], []
     for n in range(nodes):
         cp_l = pltpu.make_async_copy(l_ref.at[n], lv.at[n, pl.ds(0, block)], d_sem.at[n, 4])
         cp_l.start()
         l_in.append(cp_l)
+        if n >= 1:
+            send(LC, n, l_ref.at[n], slot(n, 1), to_core)
         for s in range(4):
             src = d_ref.at[n, :, pl.ds(pl.multiple_of(slots[s] * block, block), block)]
             one = pltpu.make_async_copy(src, dv.at[n, :, pl.ds(s * block, block)], d_sem.at[n, s])
@@ -54,64 +118,33 @@
     k_in = pltpu.make_async_copy(k_ref, kv, loc_sem.at[2])
     k_in.start()
 
-    barrier = pltpu.get_barrier_semaphore()
-    for device in (to_core, to_y, to_z):
-        pl.semaphore_signal(barrier, inc=1, device_id=device, device_id_type=MESH)
-
-    t_in.wait()
-    row_at = lax.broadcasted_iota(jnp.int32, (part, width), 0) + c * part
-    col_at = lax.broadcasted_iota(jnp.int32, (part, width), 1)
-    for n in range(nodes):
-        tw[n, rows_of(c), :] = jnp.where(row_at < ranks_ref[n], tv[n], 0.0)
-    pl.semaphore_wait(barrier, 3)
-
-    sent = []
-
-    def copy(kind, n, src, dst, device):
-        return pltpu.make_async_remote_copy(
-            src_ref=src, dst_ref=dst, send_sem=send_sem.at[kind, n], recv_sem=recv_sem.at[kind, n],
-            device_id=device, device_id_type=MESH,
-        )
-
-    def send(kind, n, src, dst, device):
-        one = copy(kind, n, src, dst, device)
-        one.start()
-        sent.append(one)
-
-    def got(kind, n, ref, device):
-        copy(kind, n, ref, ref, device).wait_recv()
-
-    def slot(n, s):
-        return lv.at[n, pl.ds(s * block, block)]
-
-    def strip(buf, n, index):
-        return buf.at[n, rows_of(index)]
-
-    for n in range(nodes):
-        send(TY, n, strip(tw, n, c), strip(tw, n, c), to_y)
-        send(LY, n, l_ref.at[n], slot(n, 2), to_y)
-        send(LC, n, l_ref.at[n], slot(n, 1), to_core)
-        send(TZ, n, strip(tw, n, c), strip(zw, n, c), to_z)
-        send(TC, n, strip(tw, n, c), strip(tw, n, c), to_core)
-
-    def times(n, first, count):
-        span = pl.ds(first * block, count * block)
+
+    def times(n, first, size):
+        span = pl.ds(first, size)
         return jnp.dot(dv[n, :, span], lv[n, span, :], preferred_element_type=jnp.float32)
 
-    def eliminate(n):
+    def relay(n):
         got(TY, n, strip(tw, n, yp), to_y)
         send(TG, n, strip(tw, n, yp), strip(zw, n, yp), to_z)
         send(TF, n, strip(tw, n, yp), strip(tw, n, yp), to_core)
+
+    def begin(n):
         l_in[n].wait()
         for s in range(4):
             d_in[4 * n + s].wait()
         got(LC, n, slot(n, 1), to_core)
-        total = times(n, 0, 2)
+        return times(n, 0, 2 * block)
+
+    def eliminate(n):
+        total = begin(n)
         got(LY, n, slot(n, 2), to_y)
         send(LF, n, slot(n, 2), slot(n, 3), to_core)
-        total = total + times(n, 2, 1)
+        total = total + times(n, 2 * block, block)
         got(LF, n, slot(n, 3), to_core)
-        total = total + times(n, 3, 1)
+        total = total + times(n, 3 * block, block)
+        skeletons(n, total)
+
+    def skeletons(n, total):
         skeleton = lax.dot_general(
             rv[n], total.astype(jnp.bfloat16), (((0,), (0,)), ((), ())), preferred_element_type=jnp.float32
         )
@@ -134,7 +167,7 @@
         got(ZG, n, strip(zw, n, slots[3]), to_core)
         got(TC, n, strip(tw, n, cp), to_core)
         got(TF, n, strip(tw, n, slots[3]), to_core)
-        mv[n] = jnp.dot(kv[n], zw[n], precision=highest, preferred_element_type=jnp.float32)
+        mv[n] = product(kv[n], zw[n], (1, 0))
 
     outs = []
 
@@ -143,12 +176,9 @@
         mine = sbuf[n, y, core] + sgot[n, y] + ygot[n].astype(jnp.float32)
         live = (row_at < ranks_ref[n]) & (col_at < ranks_ref[n])
         mine = jnp.where(live, mine, 0.0)
-        merged = mv[n] + jnp.dot(mine, tw[n], precision=highest, preferred_element_type=jnp.float32)
+        merged = mv[n] + product(mine, tw[n], (1, 0))
         mv[n] = merged
-        own = lax.dot_general(
-            tw[n, rows_of(c), :], merged, (((0,), (0,)), ((), ())), precision=highest,
-            preferred_element_type=jnp.float32,
-        )
+        own = product(tw[n, rows_of(c), :], merged, (0, 0))
         pbuf[n] = own.reshape(2, 2, part, width)
         send(PC, n, pbuf.at[n, :, 1 - core], pgot.at[n], to_core)
         one = pltpu.make_async_copy(mv.at[n], merged_ref.at[n], out_sem.at[0, n])
@@ -175,28 +205,57 @@
         outs.append(one)
 
     r_in.wait()
-    for n in range(nodes):
+    k_in.wait()
+    eliminate(0)
+    for n in range(nodes):
+        relay(n)
+    reduce_chip(0)
+    send(LY, last, l_ref.at[last, pl.ds(0, half)], piece(last, 2, 0), to_y)
+    for n in range(nodes):
+        got(TZ, n, strip(zw, n, c), to_z)
+        send(ZC, n, strip(zw, n, c), strip(zw, n, c), to_core)
+    for n in range(1, last):
         eliminate(n)
-        if n >= 1:
-            reduce_chip(n - 1)
-            hand_on_sibling(n - 1)
-    k_in.wait()
-    hand_on_sibling(nodes - 1)
-    for n in range(nodes - 1):
+        reduce_chip(n)
+    send(MY, last, l_ref.at[last, pl.ds(half, half)], piece(last, 2, half), to_y)
+
+    def hand_on(n):
+        got(TG, n, strip(zw, n, yp), to_z)
+        send(ZG, n, strip(zw, n, yp), strip(zw, n, yp), to_core)
+
+    hand_on(0)
+    couple(0)
+    merge(0)
+    total = begin(last)
+    parent_chip(0)
+    for n in range(1, last):
+        hand_on(n)
+    got(LY, last, piece(last, 2, 0), to_y)
+    send(LF, last, piece(last, 2, 0), piece(last, 3, 0), to_core)
+    total = total + times(last, 2 * block, half)
+    for n in range(1, last):
         couple(n)
-    reduce_chip(nodes - 1)
-    couple(nodes - 1)
-    for n in range(nodes):
         merge(n)
-        if n >= 1:
-            parent_chip(n - 1)
-    for n in range(nodes - 1):
+        parent_chip(n)
+    got(LF, last, piece(last, 3, 0), to_core)
+    total = total + times(last, 3 * block, half)
+    got(MY, last, piece(last, 2, half), to_y)
+    send(MF, last, piece(last, 2, half), piece(last, 3, half), to_core)
+    total = total + times(last, 2 * block + half, half)
+    got(MF, last, piece(last, 3, half), to_core)
+    total = total + times(last, 3 * block + half, half)
+    skeletons(last, total)
+    hand_on(last)
+    reduce_chip(last)
+    couple(last)
+    for n in range(last):
         parent_own(n)
-    parent_chip(nodes - 1)
-    for n in range(nodes - 1):
+    merge(last)
+    parent_chip(last)
+    for n in range(last):
         parent_all(n)
-    parent_own(nodes - 1)
-    parent_all(nodes - 1)
+    parent_own(last)
+    parent_all(last)
     for one in sent:
         one.wait_send()
     for one in outs:
@@ -207,7 +266,7 @@
     nodes, block, whole = diagonal_inverses.shape
     part, width = transfer.shape[1:]
     f32, bf16 = jnp.float32, jnp.bfloat16
-    skeleton_link, parent_link, sibling_link = f32, f32, f32
+    skeleton_link, parent_link, sibling_link = bf16, bf16, f32
     anywhere = pl.BlockSpec(memory_space=pl.ANY)
     strips = (nodes, part, width)
     square = (nodes, width, width)
@@ -239,8 +298,8 @@
             pltpu.VMEM(strips, sibling_link),
             pltpu.VMEM(strips, f32),
             pltpu.VMEM(strips, f32),
-            pltpu.SemaphoreType.DMA((15, nodes)),
-            pltpu.SemaphoreType.DMA((15, nodes)),
+            pltpu.SemaphoreType.DMA((17, nodes)),
+            pltpu.SemaphoreType.DMA((17, nodes)),
             pltpu.SemaphoreType.DMA((nodes, 5)),
             pltpu.SemaphoreType.DMA((3,)),
             pltpu.SemaphoreType.DMA((2, nodes)),

time: 55.1 us -> 50.8 us (0.922)
  Pallas kernels: 51.1 us -> 46.3 us
    pallas_call x1, Pallas kernels: 51.1 us -> 46.3 us  [shards(): pl.pallas_call(kernel, out_shape=(shape, shape), in_specs=[pl.BlockSpec(m...]
where the time goes in v2:
time: 50.8 us; the launch traced here: 50.2 us
  Pallas kernels  46.3 us (91%)
  local copies, waits for them, and re-layouts  3.23 us (6%)
  between operations  0.64 us (1%)
    pallas_call x1, Pallas kernels, shards(): pl.pallas_call(kernel, out_shape=(shape, shape), in_specs=[pl.BlockSpec(m...  46.3 us
    unnamed x2, local copies, waits for them, and re-layouts  3.23 us

profile of v2, /device:TPU:0, one launch (start us, length us, event | category | flops | bytes accessed | tf_op | source)
XLA Modules:
  0.0 50.2 jit_solution(13660788104239393701)
XLA Ops:
  0.6 46.3 %shard_map.77 = (f32[3,64,256]{2,1,0:T(8,128)}, f32[3,64,256]{2,1,0:T(8,128)}) custom-call(s32[3]{0:T(128)} %ranks_ref.1, bf16[3,512,2048]{2,1,0:T(8,128)(2,1)} %d_ref.1, bf16[3,512,256]{2,1,0:T(8,128)(2,1)} %l_ref.1, bf16[3,512,256]{2,1,0:T(8,128)(2,1)} %r_ref.1, f32[3,64,256]{2,1,0:T(8,128)} %t_ref.1, f32[3,64,256]{2,1,0:T(8,128)} %k_ref.1), custom_call_target="tpu_custom_call" | custom-call | tf_op jit(solution)/shard_map/pallas_call | solution.py:276
  46.9 1.6 %copy.10 = f32[3,64,256]{2,1,0:T(8,128)} copy(f32[3,64,256]{2,1,0:T(8,128)} %get-tuple-element.4) | data formatting | bytes 393216
  48.5 1.6 %copy.11 = f32[3,64,256]{2,1,0:T(8,128)} copy(f32[3,64,256]{2,1,0:T(8,128)} %get-tuple-element.5) | data formatting | bytes 393216

commit v3 on v2

--- a/solution.py
+++ b/solution.py
@@ -11,8 +11,8 @@
 
 
 def kernel(
-    ranks_ref, d_ref, l_ref, r_ref, t_ref, k_ref, merged_ref, parent_ref,
-    dv, lv, rv, tv, kv, tw, zw, sbuf, sgot, ysend, ygot, pbuf, pgot, pysend, pygot,
+    ranks_ref, d_ref, l_ref, r_ref, t_ref, k_ref, out_ref,
+    dv, lv, rv, tv, kv, tw, zw, sbuf, sgot, ysend, ygot, pbuf, pgot, pysend, pygot, qsend, qgot,
     esend, egot, mv, pv, send_sem, recv_sem, d_sem, loc_sem, out_sem,
 ):
     nodes, block, _ = l_ref.shape
@@ -57,57 +57,11 @@
 
     row_at = lax.broadcasted_iota(jnp.int32, (part, width), 0) + c * part
     col_at = lax.broadcasted_iota(jnp.int32, (part, width), 1)
-    pl.semaphore_wait(barrier, 3)
-
-    sent = []
-
-    def copy(kind, n, src, dst, device):
-        return pltpu.make_async_remote_copy(
-            src_ref=src, dst_ref=dst, send_sem=send_sem.at[kind, n], recv_sem=recv_sem.at[kind, n],
-            device_id=device, device_id_type=MESH,
-        )
-
-    def send(kind, n, src, dst, device):
-        one = copy(kind, n, src, dst, device)
-        one.start()
-        sent.append(one)
-
-    def got(kind, n, ref, device):
-        copy(kind, n, ref, ref, device).wait_recv()
-
-    def slot(n, s):
-        return lv.at[n, pl.ds(s * block, block)]
-
-    def strip(buf, n, index):
-        return buf.at[n, rows_of(index)]
-
-    half = block // 2
-    last = nodes - 1
-
-    def piece(n, s, first):
-        return lv.at[n, pl.ds(s * block + first, half)]
-
-    def send_basis(n):
-        send(LY, n, l_ref.at[n], slot(n, 2), to_y)
-
-    send_basis(0)
-    send(LC, 0, l_ref.at[0], slot(0, 1), to_core)
-    t_in.wait()
-    for n in range(nodes):
-        tw[n, rows_of(c), :] = jnp.where(row_at < ranks_ref[n], tv[n], 0.0)
-    for n in range(nodes):
-        send(TY, n, strip(tw, n, c), strip(tw, n, c), to_y)
-        send(TZ, n, strip(tw, n, c), strip(zw, n, c), to_z)
-        send(TC, n, strip(tw, n, c), strip(tw, n, c), to_core)
-    for n in range(1, nodes - 1):
-        send_basis(n)
     l_in, d_in = [], []
     for n in range(nodes):
         cp_l = pltpu.make_async_copy(l_ref.at[n], lv.at[n, pl.ds(0, block)], d_sem.at[n, 4])
         cp_l.start()
         l_in.append(cp_l)
-        if n >= 1:
-            send(LC, n, l_ref.at[n], slot(n, 1), to_core)
         for s in range(4):
             src = d_ref.at[n, :, pl.ds(pl.multiple_of(slots[s] * block, block), block)]
             one = pltpu.make_async_copy(src, dv.at[n, :, pl.ds(s * block, block)], d_sem.at[n, s])
@@ -117,8 +71,51 @@
     r_in.start()
     k_in = pltpu.make_async_copy(k_ref, kv, loc_sem.at[2])
     k_in.start()
-
-
+    t_in.wait()
+    for n in range(nodes):
+        tw[n, rows_of(c), :] = jnp.where(row_at < ranks_ref[n], tv[n], 0.0)
+    pl.semaphore_wait(barrier, 3)
+
+    sent = []
+
+    def copy(kind, n, src, dst, device):
+        return pltpu.make_async_remote_copy(
+            src_ref=src, dst_ref=dst, send_sem=send_sem.at[kind, n], recv_sem=recv_sem.at[kind, n],
+            device_id=device, device_id_type=MESH,
+        )
+
+    def send(kind, n, src, dst, device):
+        one = copy(kind, n, src, dst, device)
+        one.start()
+        sent.append(one)
+
+    def got(kind, n, ref, device):
+        copy(kind, n, ref, ref, device).wait_recv()
+
+    def slot(n, s):
+        return lv.at[n, pl.ds(s * block, block)]
+
+    def strip(buf, n, index):
+        return buf.at[n, rows_of(index)]
+
+    half = 3 * block // 4
+    rest = block - half
+    last = nodes - 1
+
+    def piece(n, s, first):
+        return lv.at[n, pl.ds(s * block + first, rest if first else half)]
+
+    def send_basis(n):
+        send(LY, n, l_ref.at[n], slot(n, 2), to_y)
+
+    for n in range(nodes):
+        send(TY, n, strip(tw, n, c), strip(tw, n, c), to_y)
+        send(TZ, n, strip(tw, n, c), strip(zw, n, c), to_z)
+        send(TC, n, strip(tw, n, c), strip(tw, n, c), to_core)
+    for n in range(nodes):
+        if n < last:
+            send_basis(n)
+        send(LC, n, l_ref.at[n], slot(n, 1), to_core)
     def times(n, first, size):
         span = pl.ds(first, size)
         return jnp.dot(dv[n, :, span], lv[n, span, :], preferred_element_type=jnp.float32)
@@ -155,12 +152,6 @@
         got(SC, n, sgot.at[n], to_core)
         ysend[n] = (sbuf[n, other, core] + sgot[n, other]).astype(ysend.dtype)
         send(SY, n, ysend.at[n], ygot.at[n], to_y)
-
-    def hand_on_sibling(n):
-        got(TZ, n, strip(zw, n, c), to_z)
-        send(ZC, n, strip(zw, n, c), strip(zw, n, c), to_core)
-        got(TG, n, strip(zw, n, yp), to_z)
-        send(ZG, n, strip(zw, n, yp), strip(zw, n, yp), to_core)
 
     def couple(n):
         got(ZC, n, strip(zw, n, cp), to_core)
@@ -181,18 +172,28 @@
         own = product(tw[n, rows_of(c), :], merged, (0, 0))
         pbuf[n] = own.reshape(2, 2, part, width)
         send(PC, n, pbuf.at[n, :, 1 - core], pgot.at[n], to_core)
-        one = pltpu.make_async_copy(mv.at[n], merged_ref.at[n], out_sem.at[0, n])
+        one = pltpu.make_async_copy(mv.at[n], out_ref.at[0, n], out_sem.at[0, n])
         one.start()
         outs.append(one)
 
     def parent_chip(n):
         got(PC, n, pgot.at[n], to_core)
-        pysend[n] = (pbuf[n, other, core] + pgot[n, other]).astype(pysend.dtype)
-        send(PY, n, pysend.at[n], pygot.at[n], to_y)
+        over = pbuf[n, other, core] + pgot[n, other]
+        if n < last:
+            pysend[n] = over
+            send(PY, n, pysend.at[n], pygot.at[n], to_y)
+        else:
+            qsend[...] = over.astype(qsend.dtype)
+            send(PY, n, qsend, qgot, to_y)
 
     def parent_own(n):
-        got(PY, n, pygot.at[n], to_y)
-        own = pbuf[n, y, core] + pgot[n, y] + pygot[n].astype(jnp.float32)
+        if n < last:
+            got(PY, n, pygot.at[n], to_y)
+            came = pygot[n]
+        else:
+            got(PY, n, qgot, to_y)
+            came = qgot[...].astype(jnp.float32)
+        own = pbuf[n, y, core] + pgot[n, y] + came
         pv[n] = own
         esend[n] = own.astype(esend.dtype)
         send(PZ, n, esend.at[n], egot.at[n], to_z)
@@ -200,15 +201,15 @@
     def parent_all(n):
         got(PZ, n, egot.at[n], to_z)
         pv[n] = pv[n] + egot[n].astype(jnp.float32)
-        one = pltpu.make_async_copy(pv.at[n], parent_ref.at[n], out_sem.at[1, n])
+        one = pltpu.make_async_copy(pv.at[n], out_ref.at[1, n], out_sem.at[1, n])
         one.start()
         outs.append(one)
 
     r_in.wait()
     k_in.wait()
+    for n in range(nodes):
+        relay(n)
     eliminate(0)
-    for n in range(nodes):
-        relay(n)
     reduce_chip(0)
     send(LY, last, l_ref.at[last, pl.ds(0, half)], piece(last, 2, 0), to_y)
     for n in range(nodes):
@@ -217,7 +218,7 @@
     for n in range(1, last):
         eliminate(n)
         reduce_chip(n)
-    send(MY, last, l_ref.at[last, pl.ds(half, half)], piece(last, 2, half), to_y)
+    send(MY, last, l_ref.at[last, pl.ds(half, rest)], piece(last, 2, half), to_y)
 
     def hand_on(n):
         got(TG, n, strip(zw, n, yp), to_z)
@@ -228,33 +229,37 @@
     merge(0)
     total = begin(last)
     parent_chip(0)
-    for n in range(1, last):
-        hand_on(n)
     got(LY, last, piece(last, 2, 0), to_y)
     send(LF, last, piece(last, 2, 0), piece(last, 3, 0), to_core)
     total = total + times(last, 2 * block, half)
     for n in range(1, last):
-        couple(n)
-        merge(n)
-        parent_chip(n)
+        hand_on(n)
     got(LF, last, piece(last, 3, 0), to_core)
     total = total + times(last, 3 * block, half)
     got(MY, last, piece(last, 2, half), to_y)
     send(MF, last, piece(last, 2, half), piece(last, 3, half), to_core)
-    total = total + times(last, 2 * block + half, half)
+    total = total + times(last, 2 * block + half, rest)
+    for n in range(1, last):
+        couple(n)
     got(MF, last, piece(last, 3, half), to_core)
-    total = total + times(last, 3 * block + half, half)
+    total = total + times(last, 3 * block + half, rest)
     skeletons(last, total)
+    for n in range(1, last):
+        merge(n)
+    reduce_chip(last)
+    for n in range(1, last):
+        parent_chip(n)
+    parent_own(0)
     hand_on(last)
-    reduce_chip(last)
     couple(last)
-    for n in range(last):
+    merge(last)
+    for n in range(1, last):
         parent_own(n)
-    merge(last)
     parent_chip(last)
-    for n in range(last):
+    parent_all(0)
+    parent_own(last)
+    for n in range(1, last):
         parent_all(n)
-    parent_own(last)
     parent_all(last)
     for one in sent:
         one.wait_send()
@@ -266,18 +271,17 @@
     nodes, block, whole = diagonal_inverses.shape
     part, width = transfer.shape[1:]
     f32, bf16 = jnp.float32, jnp.bfloat16
-    skeleton_link, parent_link, sibling_link = bf16, bf16, f32
+    skeleton_link, parent_link, sibling_link = bf16, f32, bf16
     anywhere = pl.BlockSpec(memory_space=pl.ANY)
     strips = (nodes, part, width)
     square = (nodes, width, width)
     quads = (nodes, 2, 2, part, width)
     pairs = (nodes, 2, part, width)
-    shape = jax.ShapeDtypeStruct(strips, f32)
-    return pl.pallas_call(
+    out = pl.pallas_call(
         kernel,
-        out_shape=(shape, shape),
+        out_shape=jax.ShapeDtypeStruct((2,) + strips, f32),
         in_specs=[pl.BlockSpec(memory_space=pltpu.SMEM)] + [anywhere] * 5,
-        out_specs=(anywhere, anywhere),
+        out_specs=anywhere,
         scratch_shapes=[
             pltpu.VMEM((nodes, block, whole), bf16),
             pltpu.VMEM((nodes, whole, width), bf16),
@@ -294,6 +298,8 @@
             pltpu.VMEM(pairs, f32),
             pltpu.VMEM(strips, parent_link),
             pltpu.VMEM(strips, parent_link),
+            pltpu.VMEM((part, width), bf16),
+            pltpu.VMEM((part, width), bf16),
             pltpu.VMEM(strips, sibling_link),
             pltpu.VMEM(strips, sibling_link),
             pltpu.VMEM(strips, f32),
@@ -306,6 +312,7 @@
         ],
         compiler_params=pltpu.CompilerParams(collective_id=0, has_side_effects=True),
     )(ranks, diagonal_inverses, column_basis, row_basis, transfer, coupling)
+    return out[0], out[1]
 
 
 def solution(mesh):

time: 50.8 us -> 46.8 us (0.921); the launches traced: 50.2 us -> 46.7 us
  Pallas kernels: 46.3 us -> 44.3 us
  local copies, waits for them, and re-layouts: 3.23 us -> 1.8 us
    unnamed x2 -> x0, local copies, waits for them, and re-layouts: 3.23 us -> none
    pallas_call x1, Pallas kernels: 46.3 us -> 44.3 us  [shards(): pl.pallas_call(kernel, out_shape=jax.ShapeDtypeStruct((2,) + strips, f32)...]
    squeeze x0 -> x1, local copies, waits for them, and re-layouts: none -> 1.8 us  [shards(): return (out[0], out[1])]
where the time goes in v3:
time: 46.8 us; the launch traced here: 46.7 us
  Pallas kernels  44.3 us (95%)
  local copies, waits for them, and re-layouts  1.8 us (4%)
  between operations  0.64 us (1%)
    pallas_call x1, Pallas kernels, shards(): pl.pallas_call(kernel, out_shape=jax.ShapeDtypeStruct((2,) + strips, f32)...  44.3 us
    squeeze x1, local copies, waits for them, and re-layouts, shards(): return (out[0], out[1])  1.8 us

profile of v3, /device:TPU:0, one launch (start us, length us, event | category | flops | bytes accessed | tf_op | source)
XLA Modules:
  0.0 46.7 jit_solution(6475674066133368811)
XLA Ops:
  0.6 44.3 %shard_map.77 = f32[2,3,64,256]{3,2,1,0:T(8,128)} custom-call(s32[3]{0:T(128)} %ranks_ref.1, bf16[3,512,2048]{2,1,0:T(8,128)(2,1)} %d_ref.1, bf16[3,512,256]{2,1,0:T(8,128)(2,1)} %l_ref.1, bf16[3,512,256]{2,1,0:T(8,128)(2,1)} %r_ref.1, f32[3,64,256]{2,1,0:T(8,128)} %t_ref.1, f32[3,64,256]{2,1,0:T(8,128)} %k_ref.1), custom_call_target="tpu_custom_call" | custom-call | tf_op jit(solution)/shard_map/pallas_call | solution.py:280
  44.9 1.8 %slice_bitcast_fusion = (f32[3,64,256]{2,1,0:T(8,128)}, f32[3,64,256]{2,1,0:T(8,128)}) fusion(f32[2,3,64,256]{3,2,1,0:T(8,128)} %shard_map.77), kind=kLoop, calls=%fused_computation | loop fusion | bytes 786432 | tf_op jit(solution)/shard_map/squeeze | solution.py:315

commit v4 on v3

--- a/solution.py
+++ b/solution.py
@@ -98,7 +98,7 @@
     def strip(buf, n, index):
         return buf.at[n, rows_of(index)]
 
-    half = 3 * block // 4
+    half = block // 2
     rest = block - half
     last = nodes - 1
 
@@ -212,13 +212,13 @@
     eliminate(0)
     reduce_chip(0)
     send(LY, last, l_ref.at[last, pl.ds(0, half)], piece(last, 2, 0), to_y)
+    send(MY, last, l_ref.at[last, pl.ds(half, rest)], piece(last, 2, half), to_y)
     for n in range(nodes):
         got(TZ, n, strip(zw, n, c), to_z)
         send(ZC, n, strip(zw, n, c), strip(zw, n, c), to_core)
     for n in range(1, last):
         eliminate(n)
         reduce_chip(n)
-    send(MY, last, l_ref.at[last, pl.ds(half, rest)], piece(last, 2, half), to_y)
 
     def hand_on(n):
         got(TG, n, strip(zw, n, yp), to_z)

time: 46.8 us -> 46.5 us (level)
  no operation moved by 1% of the time
where the time goes in v4:
time: 46.5 us; the launch traced here: 46.4 us
  Pallas kernels  43.9 us (94%)
  local copies, waits for them, and re-layouts  1.8 us (4%)
  between operations  0.64 us (1%)
    pallas_call x1, Pallas kernels, shards(): pl.pallas_call(kernel, out_shape=jax.ShapeDtypeStruct((2,) + strips, f32)...  43.9 us
    squeeze x1, local copies, waits for them, and re-layouts, shards(): return (out[0], out[1])  1.8 us

profile of v4, /device:TPU:0, one launch (start us, length us, event | category | flops | bytes accessed | tf_op | source)
XLA Modules:
  0.0 46.4 jit_solution(880408161094824522)
XLA Ops:
  0.6 43.9 %shard_map.77 = f32[2,3,64,256]{3,2,1,0:T(8,128)} custom-call(s32[3]{0:T(128)} %ranks_ref.1, bf16[3,512,2048]{2,1,0:T(8,128)(2,1)} %d_ref.1, bf16[3,512,256]{2,1,0:T(8,128)(2,1)} %l_ref.1, bf16[3,512,256]{2,1,0:T(8,128)(2,1)} %r_ref.1, f32[3,64,256]{2,1,0:T(8,128)} %t_ref.1, f32[3,64,256]{2,1,0:T(8,128)} %k_ref.1), custom_call_target="tpu_custom_call" | custom-call | tf_op jit(solution)/shard_map/pallas_call | solution.py:280
  44.6 1.8 %slice_bitcast_fusion = (f32[3,64,256]{2,1,0:T(8,128)}, f32[3,64,256]{2,1,0:T(8,128)}) fusion(f32[2,3,64,256]{3,2,1,0:T(8,128)} %shard_map.77), kind=kLoop, calls=%fused_computation | loop fusion | bytes 786432 | tf_op jit(solution)/shard_map/squeeze | solution.py:315
